TPU v7x, 32 devices: a whole 2x2x4 slice. The times are simulated.
32 devices in a mesh: store: 8 (over y, x, core), tp: 4 (over z).
Axes of the slice: x: 2, y: 2, z: 4, core: 2. Of those that a mesh axis runs over, the one named last changes fastest.
Arguments:
- hidden: bfloat16 [8, 576, 8192], P('store', None, 'tp'), may hold values from -300 to 300
- w_query: bfloat16 [8192, 4096], P(None, 'tp'), may hold values from -0.0625 to 0.0625
- w_keyvalue: bfloat16 [8192, 1024], P('tp'), may hold values from -0.1875 to 0.1875
- passage_cache: bfloat16 [32, 4, 384, 256], P('store'), may hold values from -400 to 400
- passage_ids: int32 [8, 8], replicated, may hold values from 0 to 31, as said below
- select_index: int32 [8, 576], P('store'), may hold values from 0 to 3071, as said below
- select_count: int32 [8], P('store'), may hold values from 288 to 576, as said below
Outputs:
- context: bfloat16 [8, 576, 4096], P('store', None, 'tp')
Inputs may be any that keep to these rules, and one draw needn't show every extreme that they name: `passage_ids`: the passages of one prompt lie in distinct shards of the pool, shard = id // 4. `select_index`: all entries of a row are distinct positions of the prompt; the first select_count[p] of row p are in increasing order, the others are ignored. `select_count`: some prompt of every draw has 576 selected tokens.
All inputs are finite; a program needn't handle non-finite values.
Results may differ from a plain program's by a relative error of at most 0.04.
Values may be sent and summed in bfloat16 or wider, within the bound.
No kernel may reach another device: no remote copies, remote signals or barrier semaphores. Data moves between devices by JAX's collectives and lax.ppermute only.
A program may use at most 128 MiB of HBM per device.

v0:
```python
import jax
import jax.numpy as jnp
from jax import lax
from jax.sharding import PartitionSpec as P

D = 8192
KV_HEADS = 4
HEAD_DIM = 128
PASSAGE = 384
PASSAGES = 8
SEQ = 3072
ROPE_BASE = 1000000.0
EPSILON = 1e-06


def rotate(vectors, positions):
    half_dim = vectors.shape[-1] // 2
    frequency = ROPE_BASE ** (-(jnp.arange(half_dim, dtype=jnp.float32) * 2.0) / vectors.shape[-1])
    angles = positions.astype(jnp.float32)[..., None] * frequency
    cosine = jnp.cos(angles)
    sine_part = jnp.sin(angles)
    front_half = vectors[..., :half_dim]
    back_half = vectors[..., half_dim:]
    return jnp.concatenate(
        [front_half * cosine - back_half * sine_part, back_half * cosine + front_half * sine_part],
        axis=-1,
    )


def local(hidden, w_query, w_keyvalue, passage_cache, passage_ids, select_index, select_count):
    tp_count = lax.axis_size("tp")
    group_width = tp_count // KV_HEADS
    tp_rank = lax.axis_index("tp")
    kv_head = tp_rank // group_width
    store_rank = lax.axis_index("store")
    local_heads = w_query.shape[1] // HEAD_DIM
    row_count = hidden.shape[1]
    pool_dev = passage_cache.shape[0]
    partial_kv = jnp.dot(hidden[0], w_keyvalue, preferred_element_type=jnp.float32)
    proj_kv = lax.psum(partial_kv, "tp")
    head_kv = lax.dynamic_slice_in_dim(proj_kv, kv_head * 2 * HEAD_DIM, 2 * HEAD_DIM, 1)
    token_part = lax.all_gather(hidden, "tp", axis=2, tiled=True)[0]
    widened = token_part.astype(jnp.float32)
    running = jnp.dot(token_part, w_query, preferred_element_type=jnp.float32)
    squares = jnp.sum(widened * widened, axis=-1)
    inverse_rms = lax.rsqrt(squares / D + EPSILON)
    positions = select_index[0]
    live_count = select_count[0]
    queries = rotate(
        (running * inverse_rms[:, None]).reshape(row_count, local_heads, HEAD_DIM),
        positions[:, None],
    )
    queries = (queries * HEAD_DIM ** (-0.5)).astype(jnp.bfloat16)
    key_value = head_kv * inverse_rms[:, None]
    new_keys = rotate(key_value[:, :HEAD_DIM], positions).astype(jnp.bfloat16)
    new_values = key_value[:, HEAD_DIM:].astype(jnp.bfloat16)
    head_cache = lax.dynamic_index_in_dim(passage_cache, kv_head, 1, keepdims=False)
    owners = passage_ids // pool_dev
    local_index = passage_ids % pool_dev
    matches = owners == store_rank
    local_slot = jnp.sum(jnp.where(matches, local_index, 0), axis=1)
    present = jnp.any(matches, axis=1)
    outgoing = jnp.take(head_cache, local_slot, axis=0) * present[:, None, None].astype(
        jnp.bfloat16
    )
    incoming = lax.all_to_all(outgoing, "store", split_axis=0, concat_axis=0, tiled=True)
    my_owners = lax.dynamic_index_in_dim(owners, store_rank, 0, keepdims=False)
    fetched = jnp.take(incoming, my_owners, axis=0)
    offsets = jnp.arange(PASSAGES) * PASSAGE
    old_keys = rotate(fetched[..., :HEAD_DIM].astype(jnp.float32), offsets[:, None]).astype(
        jnp.bfloat16
    )
    old_keys = old_keys.reshape(SEQ, HEAD_DIM)
    old_values = fetched[..., HEAD_DIM:].reshape(SEQ, HEAD_DIM)
    row_ids = jnp.arange(row_count, dtype=jnp.int32)
    target = jnp.where(row_ids < live_count, positions, SEQ)
    all_keys = old_keys.at[target].set(new_keys, mode="drop")
    all_values = old_values.at[target].set(new_values, mode="drop")
    allowed = jnp.arange(SEQ, dtype=jnp.int32)[None, :] <= positions[:, None]
    scores = jnp.einsum("rgd,sd->grs", queries, all_keys, preferred_element_type=jnp.float32)
    scores = jnp.where(allowed[None], scores, -jnp.inf)
    row_max = jnp.max(scores, axis=-1, keepdims=True)
    shifted = jnp.exp(scores - row_max)
    weight = (shifted / jnp.sum(shifted, axis=-1, keepdims=True)).astype(jnp.bfloat16)
    context = jnp.einsum("grs,sd->rgd", weight, all_values, preferred_element_type=jnp.float32)
    row_live = (row_ids < live_count)[:, None, None]
    context = jnp.where(row_live, context, 0.0)
    return context.reshape(1, row_count, local_heads * HEAD_DIM).astype(jnp.bfloat16)


def solution(mesh):
    in_specs = (
        P("store", None, "tp"),
        P(None, "tp"),
        P("tp", None),
        P("store", None, None, None),
        P(),
        P("store", None),
        P("store"),
    )
    out_specs = P("store", None, "tp")
    return jax.shard_map(local, mesh=mesh, in_specs=in_specs, out_specs=out_specs, check_vma=False)
```

profile of v0, /device:TPU:0, one launch (start us, length us, event | category | flops | bytes accessed | tf_op | source)
XLA Modules:
  0.0 357.8 jit_solution(9565624965004974671)
XLA Ops:
  9.4 1.8 gather_fusion
  11.2 1.3 select_multiply_fusion
  12.5 5.2 %all-to-all-start = ((bf16[8,384,256]{2,1,0:T(8,128)(2,1)}), bf16[8,384,256]{2,1,0:T(8,128)(2,1)S(1)}, u32[]{:S(2)}, u32[]{:S(2)}) async-start(bf16[8,384,256]{2,1,0:T(8,128)(2,1)} %select_multiply_fusion), calls=%async_computation | async-start | bytes 3145728 | tf_op jit(solution)/shard_map/all_to_all | solution.py:66
  17.8 7.9 %fusion.10 = f32[576,1024]{1,0:T(8,128)} fusion(bf16[2048,1024]{1,0:T(8,128)(2,1)} %param.9, bf16[1,576,2048]{2,1,0:T(8,128)(2,1)} %param.7), kind=kOutput, calls=%fused_computation.19 | convolution fusion | flops 2415919104 | bytes 8912896 | tf_op jit(solution)/shard_map/dot_general | solution.py:39
  26.7 2.6 iota_compare_fusion
  29.2 9.5 %all-to-all-done = bf16[8,384,256]{2,1,0:T(8,128)(2,1)S(1)} async-done(((bf16[8,384,256]{2,1,0:T(8,128)(2,1)}), bf16[8,384,256]{2,1,0:T(8,128)(2,1)S(1)}, u32[]{:S(2)}, u32[]{:S(2)}) %all-to-all-start) | async-done | bytes 1572896 | tf_op jit(solution)/shard_map/all_to_all | solution.py:66
  38.7 1.8 gather_fusion.1
  40.5 1.6 broadcast_select_fusion
  42.1 1.1 fusion.38
  43.9 1.3 pad_maximum_fusion
  45.2 133.2 %all-gather.2.cloned.1.call-done = bf16[1,576,8192]{2,1,0:T(8,128)(2,1)} async-done(((bf16[1,576,2048]{2,1,0:T(8,128)(2,1)}), bf16[1,576,8192]{2,1,0:T(8,128)(2,1)}) %all-gather.2.cloned.1.call-update) | async-done | bytes 9437200 | tf_op jit(solution)/shard_map/all_gather | solution.py:42
  178.4 5.8 %multiply_reduce_fusion = f32[576]{0:T(1024)S(1)} fusion(bf16[1,576,8192]{2,1,0:T(8,128)(2,1)} %all-gather.2.cloned.1.call-done), kind=kLoop, calls=%fused_computation.12 | loop fusion | flops 14155200 | bytes 9439488 | tf_op jit(solution)/shard_map/reduce_sum | solution.py:45
  185.1 13.6 %multiply_bitcast_fusion = f32[72,8,8,128]{3,1,2,0:T(8,128)S(1)} fusion(bf16[8192,1024]{1,0:T(8,128)(2,1)} %param.8, bf16[1,576,8192]{2,1,0:T(8,128)(2,1)S(1)} %copy-done.2, f32[576]{0:T(1024)S(1)} %add_rsqrt_fusion), kind=kOutput, calls=%fused_computation.24 | convolution fusion | flops 9664266240 | bytes 28576000 | tf_op jit(solution)/shard_map/dot_general | solution.py:44
  199.2 2.9 fusion.37
  202.1 71.5 %all-reduce.2.cloned.1.call-done = f32[576,1024]{1,0:T(8,128)} async-done(((f32[576,1024]{1,0:T(8,128)}), f32[576,1024]{1,0:T(8,128)}) %all-reduce.2.cloned.1.call-update) | async-done | bytes 2359312 | tf_op jit(solution)/shard_map/psum | solution.py:40
  273.6 1.2 dynamic-slice_multiply_fusion
  274.9 2.1 subtract_convert_fusion.1
  276.9 6.4 %scatter_custom_fusion = bf16[3072,128]{1,0:T(8,128)(2,1)} fusion(bf16[3072,128]{1,0:T(8,128)(2,1)} %bitcast.68, s32[576]{0:T(1024)S(1)} %fusion.32, f32[576,256]{1,0:T(8,128)S(1)} %dynamic-slice_multiply_fusion), kind=kCustom, calls=%fused_computation.43 | custom fusion | bytes 933888 | tf_op jit(solution)/shard_map/scatter | solution.py:78
  283.3 7.2 %scatter_custom_fusion.1 = bf16[3072,128]{1,0:T(8,128)(2,1)} fusion(bf16[3072,128]{1,0:T(8,128)(2,1)} %pad_maximum_fusion, s32[576]{0:T(1024)S(1)} %fusion.32, bf16[576,64]{1,0:T(8,128)(2,1)} %get-tuple-element.17, bf16[]{:T(256)} %constant.123, bf16[576,64]{1,0:T(8,128)(2,1)S(1)} %get-tuple-element.16), kind=kCustom, calls=%fused_computation.44 | custom fusion | flops 294912 | bytes 1081856 | tf_op jit(solution)/shard_map/scatter | solution.py:77
  290.5 4.7 %multiply_subtract_fusion = (f32[576,8,64]{2,0,1:T(8,128)}, f32[576,8,64]{2,0,1:T(8,128)}) fusion(f32[576,8,64]{2,1,0:T(8,128)} %get-tuple-element.11, f32[576,8,64]{2,1,0:T(8,128)S(1)} %copy-done.3, f32[576,64]{1,0:T(8,128)S(1)} %get-tuple-element.18, f32[576,64]{1,0:T(8,128)} %get-tuple-element.19), kind=kLoop, calls=%fused_computation.23 | loop fusion | flops 1769472 | bytes 5013504 | tf_op jit(solution)/shard_map/sub | solution.py:25
  295.2 28.2 %fusion.39 = (f32[8,576]{1,0:T(8,128)S(1)}, f32[8,576,3072]{2,1,0:T(8,128)}) fusion(pred[576,3072]{1,0:T(8,128)(4,1)} %iota_compare_fusion, bf16[3072,128]{1,0:T(8,128)(2,1)S(1)} %copy-done.4, f32[576,8,64]{2,0,1:T(8,128)} %get-tuple-element.9, f32[576,8,64]{2,0,1:T(8,128)} %get-tuple-element.8), kind=kOutput, calls=%fused_computation.83 | convolution fusion | flops 3668118528 | bytes 61556736 | tf_op jit(solution)/shard_map/sub | solution.py:83
  323.4 21.4 %fusion.14 = bf16[576,8,128]{2,0,1:T(8,128)(2,1)} fusion(f32[8,576,3072]{2,1,0:T(8,128)} %get-tuple-element.23, f32[8,576]{1,0:T(8,128)S(1)} %get-tuple-element.22, pred[576]{0:T(1024)(128)(4,1)S(1)} %iota_compare_fusion.1, bf16[3072,128]{1,0:T(8,128)(2,1)} %scatter_custom_fusion), kind=kOutput, calls=%fused_computation.29 | convolution fusion | flops 3653369856 | bytes 58608192 | tf_op jit(solution)/shard_map/grs,sd->rgd/dot_general | solution.py:85
  344.9 3.0 copy.12
  347.9 3.0 convert_element_type.79
  (38 shorter events, 5.1 us)
Async XLA Ops:
  6.5 1.9 copy-start
  6.5 0.8 copy-start.5
  6.5 171.9 %all-gather.2.cloned.1.call-start = ((), (), s32[]{:S(2)}) async-start(), calls=%async_computation.2 | async-start | bytes 11796480 | tf_op jit(solution)/shard_map/all_gather | solution.py:42
  12.5 26.2 %all-to-all-start = ((bf16[8,384,256]{2,1,0:T(8,128)(2,1)}), bf16[8,384,256]{2,1,0:T(8,128)(2,1)S(1)}, u32[]{:S(2)}, u32[]{:S(2)}) async-start(bf16[8,384,256]{2,1,0:T(8,128)(2,1)} %select_multiply_fusion), calls=%async_computation | async-start | bytes 3145728 | tf_op jit(solution)/shard_map/all_to_all | solution.py:66
  17.7 255.9 %all-reduce.2.cloned.1.call-start = ((), (), s32[]{:S(2)}) async-start(), calls=%async_computation.1 | async-start | bytes 4718592 | tf_op jit(solution)/shard_map/psum | solution.py:40
  25.7 0.7 copy-start.6
  178.4 6.6 %copy-start.2 = (bf16[1,576,8192]{2,1,0:T(8,128)(2,1)S(1)}, bf16[1,576,8192]{2,1,0:T(8,128)(2,1)}, u32[]{:S(2)}) copy-start(bf16[1,576,8192]{2,1,0:T(8,128)(2,1)} %all-gather.2.cloned.1.call-done) | copy-start | bytes 28311556
  202.1 88.4 %copy-start.3 = (f32[576,8,64]{2,1,0:T(8,128)S(1)}, f32[576,8,64]{2,1,0:T(8,128)}, u32[]{:S(2)}) copy-start(f32[576,8,64]{2,1,0:T(8,128)} %get-tuple-element.10) | copy-start | bytes 3538948
  290.5 4.7 %copy-start.4 = (bf16[3072,128]{1,0:T(8,128)(2,1)S(1)}, bf16[3072,128]{1,0:T(8,128)(2,1)}, u32[]{:S(2)}) copy-start(bf16[3072,128]{1,0:T(8,128)(2,1)} %scatter_custom_fusion.1) | copy-start | bytes 2359300
  323.4 27.5 %copy-start.1 = (bf16[4,4,384,256]{3,2,1,0:T(8,128)(2,1)S(1)}, bf16[4,4,384,256]{3,2,1,0:T(8,128)(2,1)}, u32[]{:S(2)}) copy-start(bf16[4,4,384,256]{3,2,1,0:T(8,128)(2,1)} %param.10) | copy-start | bytes 9437188
Sparse Core Ops, SparseCore 0:
  8.9 169.4 all-gather.1
  180.8 92.8 all-reduce.1
where the time goes:
time: 358 us
  waiting for transfers between devices  215 us (60%)
  matrix products  71.2 us (20%)
  other arithmetic  30 us (8%)
  local copies, waits for them, and re-layouts  22.3 us (6%)
  between operations  14.2 us (4%)
  starting transfers between devices  5.24 us (1%)
    all_gather x1, waiting for transfers between devices, local(): token_part = lax.all_gather(hidden, 'tp', axis=2, tiled=True)[0]  133 us
    psum x1, waiting for transfers between devices, local(): proj_kv = lax.psum(partial_kv, 'tp')  71.5 us
    sub x1, matrix products, local(): shifted = jnp.exp(scores - row_max)  28.2 us
    dot_general x1, matrix products, local(): jnp.einsum('grs,sd->rgd', weight, all_values, preferred_element_type=jnp....  21.4 us
    dot_general x1, matrix products, local(): running = jnp.dot(token_part, w_query, preferred_element_type=jnp.float32)  13.6 us
    all_to_all x1, waiting for transfers between devices, local(): lax.all_to_all(outgoing, 'store', split_axis=0, concat_axis=0, tiled=True)  9.47 us
    dot_general x1, matrix products, local(): jnp.dot(hidden[0], w_keyvalue, preferred_element_type=jnp.float32)  7.94 us
  transfers between devices with their start and end apart: 3, of which 3 were waited for; matrix products, arithmetic and copies ran while one was open for 12% of the time, Pallas kernels for 0%

commit v1 on v0

--- a/solution.py
+++ b/solution.py
@@ -37,7 +37,9 @@
     row_count = hidden.shape[1]
     pool_dev = passage_cache.shape[0]
     partial_kv = jnp.dot(hidden[0], w_keyvalue, preferred_element_type=jnp.float32)
-    proj_kv = lax.psum(partial_kv, "tp")
+    proj_kv = partial_kv
+    for hop in (1, 2):
+        proj_kv = proj_kv + lax.ppermute(proj_kv, "tp", [(dev, dev ^ hop) for dev in range(4)])
     head_kv = lax.dynamic_slice_in_dim(proj_kv, kv_head * 2 * HEAD_DIM, 2 * HEAD_DIM, 1)
     token_part = lax.all_gather(hidden, "tp", axis=2, tiled=True)[0]
     widened = token_part.astype(jnp.float32)

time: 358 us -> 407 us (1.14)
  waiting for transfers between devices: 215 us -> 256 us
  other arithmetic: 30 us -> 34.7 us
    ppermute x0 -> x2, waiting for transfers between devices: none -> 224 us  [local(): lax.ppermute(proj_kv, 'tp', [(dev, dev ^ hop) for dev in range(4)])]
    all_gather x1, waiting for transfers between devices: 133 us -> 23.6 us  [local(): token_part = lax.all_gather(hidden, 'tp', axis=2, tiled=True)[0]]
    psum x1 -> x0, waiting for transfers between devices: 71.5 us -> none  [local(): proj_kv = lax.psum(partial_kv, 'tp')]
    add x0 -> x1, other arithmetic: none -> 4.54 us  [local(): proj_kv + lax.ppermute(proj_kv, 'tp', [(dev, dev ^ hop) for dev in range(...]
  transfers between devices with their start and end apart: 3 -> 4, of which waited for: 3 -> 4; matrix products, arithmetic and copies ran while one was open for 12% -> 12% of each run, Pallas kernels for 0% -> 0%
where the time goes in v1:
time: 407 us; the launch traced here: 406 us
  waiting for transfers between devices  256 us (63%)
  matrix products  71 us (17%)
  other arithmetic  34.7 us (9%)
  local copies, waits for them, and re-layouts  22.1 us (5%)
  between operations  14.2 us (3%)
  starting transfers between devices  8.23 us (2%)
    ppermute x2, waiting for transfers between devices, local(): lax.ppermute(proj_kv, 'tp', [(dev, dev ^ hop) for dev in range(4)])  224 us
    sub x1, matrix products, local(): shifted = jnp.exp(scores - row_max)  28 us
    all_gather x1, waiting for transfers between devices, local(): token_part = lax.all_gather(hidden, 'tp', axis=2, tiled=True)[0]  23.6 us
    dot_general x1, matrix products, local(): jnp.einsum('grs,sd->rgd', weight, all_values, preferred_element_type=jnp....  21.4 us
    dot_general x1, matrix products, local(): running = jnp.dot(token_part, w_query, preferred_element_type=jnp.float32)  13.6 us
  transfers between devices with their start and end apart: 4, of which 4 were waited for; matrix products, arithmetic and copies ran while one was open for 12% of the time, Pallas kernels for 0%

profile of v1, /device:TPU:0, one launch (start us, length us, event | category | flops | bytes accessed | tf_op | source)
XLA Modules:
  0.0 406.3 jit_solution(15487141994241216393)
XLA Ops:
  9.4 1.8 gather_fusion
  12.5 5.2 %all-to-all-start = ((bf16[8,384,256]{2,1,0:T(8,128)(2,1)}), bf16[8,384,256]{2,1,0:T(8,128)(2,1)S(1)}, u32[]{:S(2)}, u32[]{:S(2)}) async-start(bf16[8,384,256]{2,1,0:T(8,128)(2,1)} %select_multiply_fusion), calls=%async_computation | async-start | bytes 3145728 | tf_op jit(solution)/shard_map/all_to_all | solution.py:68
  17.7 8.0 %fusion.10 = f32[576,1024]{1,0:T(8,128)} fusion(bf16[2048,1024]{1,0:T(8,128)(2,1)} %param.9, bf16[1,576,2048]{2,1,0:T(8,128)(2,1)} %param.7), kind=kOutput, calls=%fused_computation.19 | convolution fusion | flops 2415919104 | bytes 8912896 | tf_op jit(solution)/shard_map/dot_general | solution.py:39
  25.7 1.6 collective-permute-start
  28.2 2.6 iota_compare_fusion
  30.8 8.0 %all-to-all-done = bf16[8,384,256]{2,1,0:T(8,128)(2,1)S(1)} async-done(((bf16[8,384,256]{2,1,0:T(8,128)(2,1)}), bf16[8,384,256]{2,1,0:T(8,128)(2,1)S(1)}, u32[]{:S(2)}, u32[]{:S(2)}) %all-to-all-start) | async-done | bytes 1572896 | tf_op jit(solution)/shard_map/all_to_all | solution.py:68
  38.7 1.8 gather_fusion.1
  40.5 1.6 broadcast_select_fusion
  45.2 161.1 %collective-permute-done = f32[576,1024]{1,0:T(8,128)} collective-permute-done((f32[576,1024]{1,0:T(8,128)}, f32[576,1024]{1,0:T(8,128)}, u32[]{:S(2)}, u32[]{:S(2)}) %collective-permute-start) | collective-permute-done | bytes 2359328 | tf_op jit(solution)/shard_map/ppermute | solution.py:42
  206.3 4.5 %add.93 = f32[576,1024]{1,0:T(8,128)} add(f32[576,1024]{1,0:T(8,128)} %fusion.10, f32[576,1024]{1,0:T(8,128)} %collective-permute-done) | non-fusion elementwise | flops 589824 | bytes 7077888 | tf_op jit(solution)/shard_map/add | solution.py:42
  210.9 1.5 collective-permute-start.1
  212.3 23.6 %all-gather.2.cloned.1.call-done = bf16[1,576,8192]{2,1,0:T(8,128)(2,1)} async-done(((bf16[1,576,2048]{2,1,0:T(8,128)(2,1)}), bf16[1,576,8192]{2,1,0:T(8,128)(2,1)}) %all-gather.2.cloned.1.call-update) | async-done | bytes 9437200 | tf_op jit(solution)/shard_map/all_gather | solution.py:44
  235.9 5.8 %multiply_reduce_fusion = f32[576]{0:T(1024)S(1)} fusion(bf16[1,576,8192]{2,1,0:T(8,128)(2,1)} %all-gather.2.cloned.1.call-done), kind=kLoop, calls=%fused_computation.12 | loop fusion | flops 14155200 | bytes 9439488 | tf_op jit(solution)/shard_map/reduce_sum | solution.py:47
  242.3 13.6 %multiply_bitcast_fusion = f32[72,8,8,128]{3,1,2,0:T(8,128)S(1)} fusion(bf16[8192,1024]{1,0:T(8,128)(2,1)} %param.8, bf16[1,576,8192]{2,1,0:T(8,128)(2,1)S(1)} %copy-done.2, f32[576]{0:T(1024)S(1)} %add_rsqrt_fusion), kind=kOutput, calls=%fused_computation.24 | convolution fusion | flops 9664266240 | bytes 28576000 | tf_op jit(solution)/shard_map/dot_general | solution.py:46
  256.4 2.9 fusion.38
  259.3 62.7 %collective-permute-done.1 = f32[576,1024]{1,0:T(8,128)} collective-permute-done((f32[576,1024]{1,0:T(8,128)}, f32[576,1024]{1,0:T(8,128)}, u32[]{:S(2)}, u32[]{:S(2)}) %collective-permute-start.1) | collective-permute-done | bytes 2359328 | tf_op jit(solution)/shard_map/ppermute | solution.py:42
  323.4 2.1 subtract_convert_fusion.1
  325.4 6.6 %scatter_custom_fusion = bf16[3072,128]{1,0:T(8,128)(2,1)} fusion(bf16[3072,128]{1,0:T(8,128)(2,1)} %bitcast.68, s32[576]{0:T(1024)S(1)} %fusion.33, f32[576,256]{1,0:T(8,128)S(1)} %fusion.23), kind=kCustom, calls=%fused_computation.44 | custom fusion | bytes 933888 | tf_op jit(solution)/shard_map/scatter | solution.py:80
  332.0 7.2 %scatter_custom_fusion.1 = bf16[3072,128]{1,0:T(8,128)(2,1)} fusion(bf16[3072,128]{1,0:T(8,128)(2,1)} %pad_maximum_fusion, s32[576]{0:T(1024)S(1)} %fusion.33, bf16[576,64]{1,0:T(8,128)(2,1)} %get-tuple-element.17, bf16[]{:T(256)} %constant.123, bf16[576,64]{1,0:T(8,128)(2,1)S(1)} %get-tuple-element.16), kind=kCustom, calls=%fused_computation.45 | custom fusion | flops 294912 | bytes 1081856 | tf_op jit(solution)/shard_map/scatter | solution.py:79
  339.2 4.7 %multiply_subtract_fusion = (f32[576,8,64]{2,0,1:T(8,128)}, f32[576,8,64]{2,0,1:T(8,128)}) fusion(f32[576,8,64]{2,1,0:T(8,128)} %get-tuple-element.11, f32[576,8,64]{2,1,0:T(8,128)S(1)} %copy-done.3, f32[576,64]{1,0:T(8,128)S(1)} %get-tuple-element.18, f32[576,64]{1,0:T(8,128)} %get-tuple-element.19), kind=kLoop, calls=%fused_computation.23 | loop fusion | flops 1769472 | bytes 5013504 | tf_op jit(solution)/shard_map/sub | solution.py:25
  343.9 28.0 %fusion.40 = (f32[8,576]{1,0:T(8,128)S(1)}, f32[8,576,3072]{2,1,0:T(8,128)}) fusion(pred[576,3072]{1,0:T(8,128)(4,1)} %iota_compare_fusion, bf16[3072,128]{1,0:T(8,128)(2,1)S(1)} %copy-done.4, f32[576,8,64]{2,0,1:T(8,128)} %get-tuple-element.9, f32[576,8,64]{2,0,1:T(8,128)} %get-tuple-element.8), kind=kOutput, calls=%fused_computation.84 | convolution fusion | flops 3668118528 | bytes 61556736 | tf_op jit(solution)/shard_map/sub | solution.py:85
  371.9 21.4 %fusion.14 = bf16[576,8,128]{2,0,1:T(8,128)(2,1)} fusion(f32[8,576,3072]{2,1,0:T(8,128)} %get-tuple-element.23, f32[8,576]{1,0:T(8,128)S(1)} %get-tuple-element.22, pred[576]{0:T(1024)(128)(4,1)S(1)} %iota_compare_fusion.1, bf16[3072,128]{1,0:T(8,128)(2,1)} %scatter_custom_fusion), kind=kOutput, calls=%fused_computation.29 | convolution fusion | flops 3653369856 | bytes 58608192 | tf_op jit(solution)/shard_map/grs,sd->rgd/dot_general | solution.py:87
  393.4 3.0 copy.12
  396.4 3.0 convert_element_type.79
  (40 shorter events, 10.0 us)
Async XLA Ops:
  6.5 1.9 copy-start
  6.5 0.8 copy-start.5
  6.5 229.4 %all-gather.2.cloned.1.call-start = ((), (), s32[]{:S(2)}) async-start(), calls=%async_computation.1 | async-start | bytes 11796480 | tf_op jit(solution)/shard_map/all_gather | solution.py:44
  12.5 26.2 %all-to-all-start = ((bf16[8,384,256]{2,1,0:T(8,128)(2,1)}), bf16[8,384,256]{2,1,0:T(8,128)(2,1)S(1)}, u32[]{:S(2)}, u32[]{:S(2)}) async-start(bf16[8,384,256]{2,1,0:T(8,128)(2,1)} %select_multiply_fusion), calls=%async_computation | async-start | bytes 3145728 | tf_op jit(solution)/shard_map/all_to_all | solution.py:68
  17.7 10.3 %copy-start.6 = (s32[1,576]{1,0:T(1,128)S(1)}, s32[1,576]{1,0:T(1,128)}, u32[]{:S(2)}) copy-start(s32[1,576]{1,0:T(1,128)} %param.12) | copy-start | bytes 6916
  25.7 180.6 %collective-permute-start = (f32[576,1024]{1,0:T(8,128)}, f32[576,1024]{1,0:T(8,128)}, u32[]{:S(2)}, u32[]{:S(2)}) collective-permute-start(f32[576,1024]{1,0:T(8,128)} %fusion.10), channel_id=1, source_target_pairs={{0,1},{1,0},{2,3},{3,2},{4,5},{5,4},{6,7},{7,6},{8,9},{9,8},{10,11... | collective-permute-start | bytes 7077896 | tf_op jit(solution)/shard_map/ppermute | solution.py:42
  210.9 111.1 %collective-permute-start.1 = (f32[576,1024]{1,0:T(8,128)}, f32[576,1024]{1,0:T(8,128)}, u32[]{:S(2)}, u32[]{:S(2)}) collective-permute-start(f32[576,1024]{1,0:T(8,128)} %add.93), channel_id=1, source_target_pairs={{0,2},{1,3},{2,0},{3,1},{4,6},{5,7},{6,4},{7,5},{8,10},{9,11},{10,... | collective-permute-start | bytes 7077896 | tf_op jit(solution)/shard_map/ppermute | solution.py:42
  235.9 6.4 %copy-start.2 = (bf16[1,576,8192]{2,1,0:T(8,128)(2,1)S(1)}, bf16[1,576,8192]{2,1,0:T(8,128)(2,1)}, u32[]{:S(2)}) copy-start(bf16[1,576,8192]{2,1,0:T(8,128)(2,1)} %all-gather.2.cloned.1.call-done) | copy-start | bytes 28311556
  259.3 79.9 %copy-start.3 = (f32[576,8,64]{2,1,0:T(8,128)S(1)}, f32[576,8,64]{2,1,0:T(8,128)}, u32[]{:S(2)}) copy-start(f32[576,8,64]{2,1,0:T(8,128)} %get-tuple-element.10) | copy-start | bytes 3538948
  339.2 4.7 %copy-start.4 = (bf16[3072,128]{1,0:T(8,128)(2,1)S(1)}, bf16[3072,128]{1,0:T(8,128)(2,1)}, u32[]{:S(2)}) copy-start(bf16[3072,128]{1,0:T(8,128)(2,1)} %scatter_custom_fusion.1) | copy-start | bytes 2359300
  371.9 27.5 %copy-start.1 = (bf16[4,4,384,256]{3,2,1,0:T(8,128)(2,1)S(1)}, bf16[4,4,384,256]{3,2,1,0:T(8,128)(2,1)}, u32[]{:S(2)}) copy-start(bf16[4,4,384,256]{3,2,1,0:T(8,128)(2,1)} %param.10) | copy-start | bytes 9437188
Sparse Core Ops, SparseCore 0:
  8.9 226.9 all-gather.1
